TPU v7x, 256 devices: a whole 4x4x8 slice. The times are simulated.
256 devices in a mesh: dp: 4 (over y_lo, core), context: 64 (over y_hi, z, x).
Axes of the slice: x: 4, y: 4 (y_hi: 2, y_lo: 2; y = y_hi * 2 + y_lo), z: 8, core: 2. Of those that a mesh axis runs over, the one named last changes fastest.
Arguments:
- queries: bfloat16 [4, 1024, 8192], P('dp', None, 'context'), may hold values from -6 to 6
- key_stream: bfloat16 [4, 1024, 8192], P('dp', None, 'context'), may hold values from -6 to 6
- value_stream: bfloat16 [4, 1024, 8192], P('dp', None, 'context'), may hold values from -6 to 6
- cotangent: bfloat16 [4, 1024, 8192], P('dp', None, 'context'), may hold values from -6 to 6
- short_taps: float32 [3, 3, 1024], replicated, may hold values from -2 to 2
- residues: float32 [1024, 16], P('context'), may hold values from -1.5 to 1.5
- decay_rates: float32 [1024, 16], P('context'), as said below
Outputs:
- output: bfloat16 [4, 1024, 8192], P('dp', None, 'context')
- adjoint_queries: bfloat16 [4, 1024, 8192], P('dp', None, 'context')
- adjoint_keys: bfloat16 [4, 1024, 8192], P('dp', None, 'context')
- adjoint_values: bfloat16 [4, 1024, 8192], P('dp', None, 'context')
- adjoint_taps: float32 [3, 3, 1024], replicated
- adjoint_residues: float32 [1024, 16], P('context')
- adjoint_decays: float32 [1024, 16], P('context')
Inputs may be any that keep to these rules, and one draw needn't show every extreme that they name: `decay_rates`: every rate lies between 1 / 16384 and 0.05.
All inputs are finite; a program needn't handle non-finite values.
Results may differ from a plain program's by a relative error of at most 0.017.
Values may be sent and summed in bfloat16 or wider, within the bound.
A program may use at most 128 MiB of HBM per device.

v0:
```python
import math
import jax
import jax.numpy as jnp
from jax import lax
from jax.sharding import PartitionSpec as P

HIGHEST_PRECISION = lax.Precision.HIGHEST


def passed_along(x, axis, by):
    peers = lax.axis_size(axis)
    pairs = [(i, i + by) for i in range(peers) if 0 <= i + by < peers]
    return lax.ppermute(x, axis, pairs)


def dft_tables(seq_length):
    total_len = 2 * seq_length
    col_count = min(256, seq_length)
    row_count = total_len // col_count
    half_rows = row_count // 2
    row_index = jnp.arange(row_count, dtype=jnp.int32)
    half_index = jnp.arange(half_rows, dtype=jnp.int32)
    col_index = jnp.arange(col_count, dtype=jnp.int32)
    first_angle = (row_index[:, None] * half_index[None, :] % row_count).astype(jnp.float32) * (
        2.0 * math.pi / row_count
    )
    twist_angle = (row_index[:, None] * col_index[None, :] % total_len).astype(jnp.float32) * (
        2.0 * math.pi / total_len
    )
    second_angle = (col_index[:, None] * col_index[None, :] % col_count).astype(jnp.float32) * (
        2.0 * math.pi / col_count
    )
    return (
        jnp.cos(first_angle),
        jnp.sin(first_angle),
        jnp.cos(twist_angle),
        jnp.sin(twist_angle),
        jnp.cos(second_angle),
        jnp.sin(second_angle),
    )


def along_cols(array, table):
    return jnp.einsum("bckm,mj->bckj", array, table, precision=HIGHEST_PRECISION)


def forward_dft(signal, tables):
    cos_first, sin_first, cos_twist, sin_twist, cos_second, sin_second = tables
    batch_here, chan_here, seq_length = signal.shape
    folded = signal.reshape(batch_here, chan_here, cos_first.shape[1], cos_second.shape[0])
    part_re = jnp.einsum("kn,bcnm->bckm", cos_first, folded, precision=HIGHEST_PRECISION)
    part_im = -jnp.einsum("kn,bcnm->bckm", sin_first, folded, precision=HIGHEST_PRECISION)
    twist_re = part_re * cos_twist + part_im * sin_twist
    twist_im = part_im * cos_twist - part_re * sin_twist
    spec_re = along_cols(twist_re, cos_second) + along_cols(twist_im, sin_second)
    spec_im = along_cols(twist_im, cos_second) - along_cols(twist_re, sin_second)
    return (spec_re, spec_im)


def inverse_dft(spec_re, spec_im, tables):
    cos_first, sin_first, cos_twist, sin_twist, cos_second, sin_second = tables
    back_re = along_cols(spec_re, cos_second) - along_cols(spec_im, sin_second)
    back_im = along_cols(spec_im, cos_second) + along_cols(spec_re, sin_second)
    turn_re = back_re * cos_twist - back_im * sin_twist
    turn_im = back_im * cos_twist + back_re * sin_twist
    folded = jnp.einsum(
        "kn,bckm->bcnm", cos_first, turn_re, precision=HIGHEST_PRECISION
    ) - jnp.einsum("kn,bckm->bcnm", sin_first, turn_im, precision=HIGHEST_PRECISION)
    batch_here, chan_here, half_rows, col_count = folded.shape
    return folded.reshape(batch_here, chan_here, half_rows * col_count) / (
        2.0 * half_rows * col_count
    )


def freq_grid(seq_length, tables):
    row_count = tables[2].shape[0]
    col_count = tables[2].shape[1]
    total_len = 2 * seq_length
    freq_index = (
        jnp.arange(row_count, dtype=jnp.int32)[:, None]
        + row_count * jnp.arange(col_count, dtype=jnp.int32)[None, :]
    )
    signed_index = jnp.where(freq_index >= seq_length, freq_index - total_len, freq_index)
    angle = signed_index.astype(jnp.float32) * (2.0 * math.pi / total_len)
    half_sine = jnp.sin(0.5 * angle)
    return (half_sine * half_sine, jnp.sin(angle), freq_index % 2 == 0)


def mode_response(decay, half_square, sine, is_even, seq_length):
    damping = jnp.exp(-decay)
    amplitude = jnp.sqrt(-jnp.expm1(-2.0 * decay))
    numerator = jnp.where(
        is_even, -jnp.expm1(-decay * seq_length), 1.0 + jnp.exp(-decay * seq_length)
    )
    real_den = -jnp.expm1(-decay) + 2.0 * damping * half_square
    imag_den = damping * sine
    factor = amplitude * numerator / (real_den * real_den + imag_den * imag_den)
    return (factor * real_den, -factor * imag_den)


def filter_spectrum(residues, decay_rates, grid, seq_length):
    half_square, sine, is_even = grid

    def add_mode(carry, inputs):
        residue_col, decay_col = inputs
        resp_re, resp_im = mode_response(
            decay_col[:, None, None], half_square, sine, is_even, seq_length
        )
        weight_col = residue_col[:, None, None]
        return ((carry[0] + weight_col * resp_re, carry[1] + weight_col * resp_im), None)

    empty = jnp.zeros((residues.shape[0],) + sine.shape, jnp.float32)
    spectra, unused = lax.scan(add_mode, (empty, empty), (residues.T, decay_rates.T))
    return spectra


def mode_adjoints(residues, decay_rates, adj_re, adj_im, grid, seq_length):
    half_square, sine, is_even = grid

    def one_mode(carry, inputs):
        residue_col, decay_col = inputs
        decay_cube = decay_col[:, None, None]

        def response(decay_value):
            return mode_response(decay_value, half_square, sine, is_even, seq_length)

        values, tangents = jax.jvp(response, (decay_cube,), (jnp.ones_like(decay_cube),))
        residue_term = jnp.sum(adj_re * values[0] + adj_im * values[1], axis=(1, 2))
        decay_term = (
            jnp.sum(adj_re * tangents[0] + adj_im * tangents[1], axis=(1, 2))
            * residue_col
            * decay_col
        )
        return (carry, (residue_term, decay_term))

    unused, terms = lax.scan(one_mode, jnp.zeros((), jnp.float32), (residues.T, decay_rates.T))
    return (terms[0].T, terms[1].T)


def owner_work(gated, upstream, residues, decay_rates):
    seq_length = gated.shape[2]
    tables = dft_tables(seq_length)
    grid = freq_grid(seq_length, tables)
    spec_re, spec_im = filter_spectrum(residues, decay_rates, grid, seq_length)

    def convolve(signal, filt_re, filt_im):
        sig_re, sig_im = forward_dft(signal, tables)
        return inverse_dft(
            sig_re * filt_re - sig_im * filt_im, sig_re * filt_im + sig_im * filt_re, tables
        )

    mixed_exact, pullback = jax.vjp(convolve, gated.astype(jnp.float32), spec_re, spec_im)
    source_adj, adj_re, adj_im = pullback(upstream.astype(jnp.float32))
    residue_adj, decay_adj = mode_adjoints(residues, decay_rates, adj_re, adj_im, grid, seq_length)
    return (
        mixed_exact.astype(jnp.bfloat16),
        source_adj.astype(jnp.bfloat16),
        residue_adj,
        decay_adj,
    )


def featurize(extended, weights, length_here):
    reach_back = weights.shape[0] - 1
    result = jnp.zeros(extended[:, :, :length_here].shape, jnp.float32)
    for offset in range(reach_back + 1):
        start_at = reach_back - offset
        result = (
            result
            + weights[offset][None, :, None] * extended[:, :, start_at : start_at + length_here]
        )
    return result


def per_device(queries, key_stream, value_stream, cotangent, short_taps, residues, decay_rates):
    reach_back = short_taps.shape[1] - 1
    length_here = queries.shape[2]
    rim_parts = passed_along(
        (
            queries[:, :, length_here - reach_back :],
            key_stream[:, :, length_here - reach_back :],
            value_stream[:, :, length_here - reach_back :],
        ),
        "context",
        1,
    )
    extended = [
        jnp.concatenate([rim_part, signal], axis=2).astype(jnp.float32)
        for signal, rim_part in zip((queries, key_stream, value_stream), rim_parts)
    ]
    query_short, key_short, value_short = [
        featurize(extended[stream], short_taps[stream], length_here).astype(jnp.bfloat16)
        for stream in range(3)
    ]
    upstream = (cotangent.astype(jnp.float32) * query_short.astype(jnp.float32)).astype(
        jnp.bfloat16
    )
    key_own, value_own, upstream_own = (
        lax.all_to_all(key_short, "context", split_axis=1, concat_axis=2, tiled=True),
        lax.all_to_all(value_short, "context", split_axis=1, concat_axis=2, tiled=True),
        lax.all_to_all(upstream, "context", split_axis=1, concat_axis=2, tiled=True),
    )
    gated_own = (key_own.astype(jnp.float32) * value_own.astype(jnp.float32)).astype(jnp.bfloat16)
    mixed_own, source_own, residue_adj, decay_adj = owner_work(
        gated_own, upstream_own, residues, decay_rates
    )
    key_adj_own = (source_own.astype(jnp.float32) * value_own.astype(jnp.float32)).astype(
        jnp.bfloat16
    )
    value_adj_own = (source_own.astype(jnp.float32) * key_own.astype(jnp.float32)).astype(
        jnp.bfloat16
    )
    mixed_seq, key_adj, value_adj = (
        lax.all_to_all(mixed_own, "context", split_axis=2, concat_axis=1, tiled=True),
        lax.all_to_all(key_adj_own, "context", split_axis=2, concat_axis=1, tiled=True),
        lax.all_to_all(value_adj_own, "context", split_axis=2, concat_axis=1, tiled=True),
    )
    output = (query_short.astype(jnp.float32) * mixed_seq.astype(jnp.float32)).astype(jnp.bfloat16)
    query_adj = (cotangent.astype(jnp.float32) * mixed_seq.astype(jnp.float32)).astype(jnp.bfloat16)
    stream_adjs = (query_adj, key_adj, value_adj)
    next_parts = passed_along(
        (query_adj[:, :, :reach_back], key_adj[:, :, :reach_back], value_adj[:, :, :reach_back]),
        "context",
        -1,
    )
    signal_adjs = []
    tap_rows = []
    for stream in range(3):
        adjoint_f = stream_adjs[stream].astype(jnp.float32)
        ahead = jnp.concatenate([stream_adjs[stream], next_parts[stream]], axis=2).astype(
            jnp.float32
        )
        total_adj = jnp.zeros(adjoint_f.shape, jnp.float32)
        per_tap = []
        for offset in range(reach_back + 1):
            total_adj = (
                total_adj
                + short_taps[stream, offset][None, :, None]
                * ahead[:, :, offset : offset + length_here]
            )
            start_at = reach_back - offset
            per_tap.append(
                jnp.sum(
                    adjoint_f * extended[stream][:, :, start_at : start_at + length_here],
                    axis=(0, 2),
                )
            )
        signal_adjs.append(total_adj.astype(jnp.bfloat16))
        tap_rows.append(jnp.stack(per_tap))
    tap_part = jnp.stack(tap_rows)
    token_scale = 1.0 / math.sqrt(
        queries.shape[0] * lax.axis_size("dp") * length_here * lax.axis_size("context")
    )
    tap_total = lax.psum(tap_part, ("dp", "context"))
    residue_own, decay_own = lax.psum((residue_adj, decay_adj), "dp")
    return (
        output,
        signal_adjs[0],
        signal_adjs[1],
        signal_adjs[2],
        tap_total * token_scale,
        residue_own * token_scale,
        decay_own * token_scale,
    )


def solution(mesh):
    in_specs = (
        P("dp", None, "context"),
        P("dp", None, "context"),
        P("dp", None, "context"),
        P("dp", None, "context"),
        P(),
        P("context", None),
        P("context", None),
    )
    out_specs = (
        P("dp", None, "context"),
        P("dp", None, "context"),
        P("dp", None, "context"),
        P("dp", None, "context"),
        P(),
        P("context", None),
        P("context", None),
    )
    return jax.shard_map(
        per_device, mesh=mesh, in_specs=in_specs, out_specs=out_specs, check_vma=False
    )
```

profile of v0, /device:TPU:230, one launch (start us, length us, event | category | flops | bytes accessed | tf_op | source)
XLA Modules:
  0.0 640.2 jit_solution(5047321556675018098)
XLA Ops:
  4.7 7.0 %collective-permute-done.1 = bf16[1,1024,2]{2,1,0:T(8,128)(2,1)S(1)} collective-permute-done((bf16[1,1024,2]{2,1,0:T(8,128)(2,1)S(1)}, bf16[1,1024,2]{2,1,0:T(8,128)(2,1)S(1)}, u32[]{:S(2)}, u32[]{:S(2)}) %collective-permute-start.1) | collective-permute-done | bytes 4128 | tf_op jit(solution)/shard_map/ppermute | solution.py:13
  15.7 2.2 reduce
  18.7 12.4 %all-to-all-start = ((bf16[64,2,1024]{2,1,0:T(2,128)(2,1)}), bf16[64,2,1024]{2,1,0:T(2,128)(2,1)S(1)}, u32[]{:S(2)}, u32[]{:S(2)}) async-start(bf16[64,2,1024]{2,1,0:T(2,128)(2,1)} %reshape.877), calls=%async_computation | async-start | bytes 524288 | tf_op jit(solution)/shard_map/all_to_all | solution.py:199
  31.3 4.9 collective-permute-start.2
  37.1 3.4 collective-permute-start
  44.2 2.3 reduce.1
  47.2 13.0 %all-to-all-start.1 = ((bf16[64,2,1024]{2,1,0:T(2,128)(2,1)}), bf16[64,2,1024]{2,1,0:T(2,128)(2,1)S(1)}, u32[]{:S(2)}, u32[]{:S(2)}) async-start(bf16[64,2,1024]{2,1,0:T(2,128)(2,1)} %reshape.879), calls=%async_computation.1 | async-start | bytes 524288 | tf_op jit(solution)/shard_map/all_to_all | solution.py:200
  60.3 47.8 %while.33 = (s32[]{:T(128)}, f32[16,64,256]{2,1,0:T(8,128)S(1)}, f32[16,64,256]{2,1,0:T(8,128)S(1)}, f32[16,16]{1,0:T(8,128)}, f32[16,16]{1,0:T(8,128)}, /*index=5*/s32[256]{0:T(256)S(1)}, s32[]{:T(128)}, s32[]{:T(128)}) while((s32[]{:T(128)}, f32[16,64,256]{2,1,0:T(8,128)S(1)}, ...), condition=%wide.region_1.2_spmd.clone.clone.clone, body=%wide.region_0.1_spmd.clone.clone.clone.sunk | while | flops 5062803 | bytes 4492583 | solution.py:113
  113.7 2.3 reduce.2
  116.8 13.0 %all-to-all-start.3 = ((bf16[64,2,1024]{2,1,0:T(2,128)(2,1)}), bf16[64,2,1024]{2,1,0:T(2,128)(2,1)}, u32[]{:S(2)}, u32[]{:S(2)}) async-start(bf16[64,2,1024]{2,1,0:T(2,128)(2,1)} %reshape.883), calls=%async_computation.3 | async-start | bytes 524288 | tf_op jit(solution)/shard_map/all_to_all | solution.py:201
  134.9 4.8 all-to-all-done.3
  139.7 3.1 reshape.884
  147.3 2.1 convolution_bitcast_fusion
  149.5 2.2 convolution_bitcast_fusion.1
  159.8 2.2 convolution_add_fusion.5
  166.0 3.9 multiply_add_fusion.3
  169.9 3.0 fusion.132
  172.9 3.2 fusion.77
  187.7 6.7 %copy.214 = bf16[1,16,8192]{1,0,2:T(2,128)(2,1)} copy(bf16[1,16,8192]{2,1,0:T(8,128)(2,1)S(1)} %convert_element_type.446) | data formatting | bytes 524288 | tf_op jit(solution)/shard_map/convert_element_type | solution.py:156
  194.4 47.1 %reduce.3 = bf16[8192,16]{1,0:T(8,128)(2,1)} reduce(bf16[8192,1,16]{2,1,0:T(2,128)(2,1)} %bitcast.310, bf16[]{:T(256)} %broadcast.596), dimensions={1}, to_apply=%bitcast.253.reduce_sub_computation | reduce | bytes 524290
  241.5 4.4 reshape.881
  245.9 8.5 %all-to-all-start.2 = ((bf16[64,2,1024]{2,1,0:T(2,128)(2,1)}), bf16[64,2,1024]{2,1,0:T(2,128)(2,1)S(1)}, u32[]{:S(2)}, u32[]{:S(2)}) async-start(bf16[64,2,1024]{2,1,0:T(2,128)(2,1)} %reshape.881), calls=%async_computation.2 | async-start | bytes 524288 | tf_op jit(solution)/shard_map/all_to_all | solution.py:214
  254.4 3.2 convolution_add_fusion.1
  257.6 3.2 convolution_add_fusion
  262.7 2.7 copy.231
  265.3 2.6 copy.221
  267.9 2.6 copy.225
  270.6 9.7 %multiply_convert_fusion = (bf16[1,16,8192]{1,0,2:T(2,128)(2,1)}, bf16[1,16,8192]{1,0,2:T(2,128)(2,1)}) fusion(f32[1,16,8192]{1,0,2:T(1,128)} %bitcast.306, f32[1,16,8192]{1,0,2:T(1,128)} %bitcast.308, f32[1,16,8192]{1,0,2:T(1,128)} %bitcast.307), kind=kLoop, calls=%fused_computation.90 | loop fusion | flops 524288 | bytes 2097152 | tf_op jit(solution)/shard_map/convert_element_type | solution.py:210
  280.3 46.9 %reduce.4 = bf16[8192,16]{1,0:T(8,128)(2,1)} reduce(bf16[8192,1,16]{2,1,0:T(2,128)(2,1)} %bitcast.309, bf16[]{:T(256)} %broadcast.596), dimensions={1}, to_apply=%bitcast.257.reduce_sub_computation | reduce | bytes 524290
  327.2 4.4 reshape.885
  331.6 13.4 %all-to-all-start.4 = ((bf16[64,2,1024]{2,1,0:T(2,128)(2,1)}), bf16[64,2,1024]{2,1,0:T(2,128)(2,1)}, u32[]{:S(2)}, u32[]{:S(2)}) async-start(bf16[64,2,1024]{2,1,0:T(2,128)(2,1)} %reshape.885), calls=%async_computation.4 | async-start | bytes 524288 | tf_op jit(solution)/shard_map/all_to_all | solution.py:215
  345.1 67.6 %while.32 = (s32[]{:T(128)}, f32[16,16]{1,0:T(8,128)S(1)}, f32[16,16]{1,0:T(8,128)S(1)}, f32[16,16]{1,0:T(8,128)}, f32[16,64,256]{2,1,0:T(8,128)S(1)}, /*index=5...) while((s32[]{:T(128)}, f32[16,16]{1,0:T(8,128)S(1)}, ...), condition=%wide.region_15.16_spmd.clone.clone.clone, body=%wide.region_12.15_spmd.clone.clone.clone.sunk | while | flops 12403026 | bytes 2396661 | solution.py:136
  346.3 2.2 fusion.310
  350.6 2.2 fusion.310
  354.8 2.2 fusion.310
  359.0 2.2 fusion.310
  363.2 2.2 fusion.310
  367.5 2.2 fusion.310
  371.7 2.2 fusion.310
  375.9 2.2 fusion.310
  380.1 2.2 fusion.310
  384.4 2.2 fusion.310
  388.6 2.2 fusion.310
  392.8 2.2 fusion.310
  397.0 2.2 fusion.310
  401.3 2.2 fusion.310
  405.5 2.2 fusion.310
  409.7 2.2 fusion.310
  412.8 45.3 %reduce.5 = bf16[8192,16]{1,0:T(8,128)(2,1)S(1)} reduce(bf16[8192,1,16]{2,1,0:T(2,128)(2,1)} %bitcast.305, bf16[]{:T(256)} %broadcast.596), dimensions={1}, to_apply=%bitcast.259.reduce_sub_computation | reduce | bytes 524290
  458.1 2.9 reshape.887
  461.0 10.4 %all-reduce = (f32[16,16]{1,0:T(8,128)S(1)}, f32[16,16]{1,0:T(8,128)S(1)}) all-reduce(f32[16,16]{1,0:T(8,128)S(1)} %bitcast.355, f32[16,16]{1,0:T(8,128)S(1)} %bitcast.356), channel_id=1, replica_groups=mesh['dp'=4,'context'=64] {'dp'}, use_global_device_ids=true, to_apply=%region_16.17 | all-reduce | flops 512 | bytes 4096 | tf_op jit(solution)/shard_map/psum | solution.py:255
  472.6 7.6 %reshape.882 = bf16[8192,1,16]{2,1,0:T(2,128)(2,1)} reshape(bf16[64,2,1024]{2,1,0:T(2,128)(2,1)S(1)} %all-to-all-done.2) | data formatting | bytes 524288
  480.2 7.9 %copy.215 = bf16[1,16,8192]{2,1,0:T(8,128)(2,1)S(1)} copy(bf16[1,16,8192]{1,0,2:T(2,128)(2,1)} %bitcast.311) | data formatting | bytes 524288 | tf_op jit(solution)/shard_map/all_to_all | solution.py:214
  488.1 13.0 %all-to-all-start.5 = ((bf16[64,2,1024]{2,1,0:T(2,128)(2,1)}), bf16[64,2,1024]{2,1,0:T(2,128)(2,1)S(1)}, u32[]{:S(2)}, u32[]{:S(2)}) async-start(bf16[64,2,1024]{2,1,0:T(2,128)(2,1)} %reshape.887), calls=%async_computation.5 | async-start | bytes 524288 | tf_op jit(solution)/shard_map/all_to_all | solution.py:216
  501.6 9.9 %reshape.886 = bf16[8192,1,16]{2,1,0:T(2,128)(2,1)} reshape(bf16[64,2,1024]{2,1,0:T(2,128)(2,1)} %all-to-all-done.4) | data formatting | bytes 524288
  511.4 7.9 %copy.223 = bf16[1,16,8192]{2,1,0:T(8,128)(2,1)S(1)} copy(bf16[1,16,8192]{1,0,2:T(2,128)(2,1)} %bitcast.312) | data formatting | bytes 524288 | tf_op jit(solution)/shard_map/all_to_all | solution.py:215
  520.3 7.6 %reshape.888 = bf16[8192,1,16]{2,1,0:T(2,128)(2,1)} reshape(bf16[64,2,1024]{2,1,0:T(2,128)(2,1)S(1)} %all-to-all-done.5) | data formatting | bytes 524288
  528.0 8.0 %copy.227 = bf16[1,16,8192]{2,1,0:T(8,128)(2,1)S(1)} copy(bf16[1,16,8192]{1,0,2:T(2,128)(2,1)} %bitcast.313) | data formatting | bytes 524288 | tf_op jit(solution)/shard_map/all_to_all | solution.py:216
  537.1 2.5 fusion.91
  539.6 75.4 %psum.21 = f32[3,3,1024]{2,1,0:T(4,128)S(1)} all-reduce(f32[3,3,1024]{2,1,0:T(4,128)S(1)} %pad_maximum_fusion), channel_id=1, replica_groups=mesh['dp'=4,'context'=64] {'dp','context'}, use_global_device_ids=true, to_apply=%region_11.12 | all-reduce | flops 9216 | bytes 73728 | tf_op jit(solution)/shard_map/psum | solution.py:254
  617.6 3.3 collective-permute-start.4
  621.1 2.6 collective-permute-start.3
  623.7 8.1 %collective-permute-done.5 = bf16[1,1024,2]{2,1,0:T(8,128)(2,1)S(1)} collective-permute-done((bf16[1,1024,2]{2,1,0:T(8,128)(2,1)S(1)}, bf16[1,1024,2]{2,1,0:T(8,128)(2,1)S(1)}, u32[]{:S(2)}, u32[]{:S(2)}) %collective-permute-start.5) | collective-permute-done | bytes 4128 | tf_op jit(solution)/shard_map/ppermute | solution.py:13
  633.4 3.0 collective-permute-done.4
  (390 shorter events, 145.6 us)
Async XLA Ops:
  0.6 30.5 %copy-start.19 = (bf16[1,1024,128]{2,1,0:T(8,128)(2,1)S(1)}, bf16[1,1024,128]{2,1,0:T(8,128)(2,1)}, u32[]{:S(2)}) copy-start(bf16[1,1024,128]{2,1,0:T(8,128)(2,1)} %param.13) | copy-start | bytes 786436
  0.6 35.5 %copy-start.20 = (bf16[1,1024,128]{2,1,0:T(8,128)(2,1)S(1)}, bf16[1,1024,128]{2,1,0:T(8,128)(2,1)}, u32[]{:S(2)}) copy-start(bf16[1,1024,128]{2,1,0:T(8,128)(2,1)} %param.11) | copy-start | bytes 786436
  0.7 39.8 %copy-start.33 = (f32[16,16]{1,0:T(8,128)S(1)}, f32[16,16]{1,0:T(8,128)}, u32[]{:S(2)}) copy-start(f32[16,16]{1,0:T(8,128)} %param.16) | copy-start | bytes 3076
  0.7 40.5 %copy-start.34 = (f32[16,16]{1,0:T(8,128)S(1)}, f32[16,16]{1,0:T(8,128)}, u32[]{:S(2)}) copy-start(f32[16,16]{1,0:T(8,128)} %param.17) | copy-start | bytes 3076
  1.8 9.9 %collective-permute-start.1 = (bf16[1,1024,2]{2,1,0:T(8,128)(2,1)S(1)}, bf16[1,1024,2]{2,1,0:T(8,128)(2,1)S(1)}, u32[]{:S(2)}, u32[]{:S(2)}) collective-permute-start(bf16[1,1024,2]{2,1,0:T(8,128)(2,1)S(1)} %slice.146), channel_id=1, source_target_pairs={{0,1},{1,2},{2,3},{3,4},{4,5},{5,6},{6,7},{7,8},{8,9},{9,10},{10,1... | collective-permute-start | bytes 12296 | tf_op jit(solution)/shard_map/ppermute | solution.py:13
  4.7 26.4 %copy-start.21 = (f32[1,1,1024]{2,1,0:T(1,128)}, f32[1,1,1024]{2,1,0:T(1,128)S(1)}, u32[]{:S(2)}) copy-start(f32[1,1,1024]{2,1,0:T(1,128)S(1)} %get-tuple-element.452) | copy-start | bytes 12292
  4.7 26.4 %copy-start.23 = (f32[1,1,1024]{2,1,0:T(1,128)}, f32[1,1,1024]{2,1,0:T(1,128)S(1)}, u32[]{:S(2)}) copy-start(f32[1,1,1024]{2,1,0:T(1,128)S(1)} %get-tuple-element.453) | copy-start | bytes 12292
  4.7 26.4 %copy-start.25 = (f32[1,1,1024]{2,1,0:T(1,128)}, f32[1,1,1024]{2,1,0:T(1,128)S(1)}, u32[]{:S(2)}) copy-start(f32[1,1,1024]{2,1,0:T(1,128)S(1)} %get-tuple-element.454) | copy-start | bytes 12292
  4.7 37.4 %copy-start.27 = (f32[1,1,1024]{2,1,0:T(1,128)}, f32[1,1,1024]{2,1,0:T(1,128)S(1)}, u32[]{:S(2)}) copy-start(f32[1,1,1024]{2,1,0:T(1,128)S(1)} %get-tuple-element.451) | copy-start | bytes 12292
  4.7 37.4 %copy-start.29 = (f32[1,1,1024]{2,1,0:T(1,128)}, f32[1,1,1024]{2,1,0:T(1,128)S(1)}, u32[]{:S(2)}) copy-start(f32[1,1,1024]{2,1,0:T(1,128)S(1)} %get-tuple-element.458) | copy-start | bytes 12292
  4.7 37.4 %copy-start.31 = (f32[1,1,1024]{2,1,0:T(1,128)}, f32[1,1,1024]{2,1,0:T(1,128)S(1)}, u32[]{:S(2)}) copy-start(f32[1,1,1024]{2,1,0:T(1,128)S(1)} %get-tuple-element.459) | copy-start | bytes 12292
  12.9 1.0 copy-start.4
  18.7 28.5 %all-to-all-start = ((bf16[64,2,1024]{2,1,0:T(2,128)(2,1)}), bf16[64,2,1024]{2,1,0:T(2,128)(2,1)S(1)}, u32[]{:S(2)}, u32[]{:S(2)}) async-start(bf16[64,2,1024]{2,1,0:T(2,128)(2,1)} %reshape.877), calls=%async_computation | async-start | bytes 524288 | tf_op jit(solution)/shard_map/all_to_all | solution.py:199
  31.3 10.5 %collective-permute-start.2 = (bf16[1,1024,2]{2,1,0:T(8,128)(2,1)S(1)}, bf16[1,1024,2]{2,1,0:T(8,128)(2,1)S(1)}, u32[]{:S(2)}, u32[]{:S(2)}) collective-permute-start(bf16[1,1024,2]{2,1,0:T(8,128)(2,1)S(1)} %slice.153), channel_id=1, source_target_pairs={{0,1},{1,2},{2,3},{3,4},{4,5},{5,6},{6,7},{7,8},{8,9},{9,10},{10,1... | collective-permute-start | bytes 12296 | tf_op jit(solution)/shard_map/ppermute | solution.py:13
  37.1 71.1 %collective-permute-start = (bf16[1,1024,2]{1,2,0:T(2,128)(2,1)}, bf16[1,1024,2]{1,2,0:T(2,128)(2,1)}, u32[]{:S(2)}, u32[]{:S(2)}) collective-permute-start(bf16[1,1024,2]{1,2,0:T(2,128)(2,1)} %copy.232), channel_id=1, source_target_pairs={{0,1},{1,2},{2,3},{3,4},{4,5},{5,6},{6,7},{7,8},{8,9},{9,10},{10,1... | collective-permute-start | bytes 12296 | tf_op jit(solution)/shard_map/ppermute | solution.py:13
  42.1 1.0 copy-start.6
  47.2 69.6 %all-to-all-start.1 = ((bf16[64,2,1024]{2,1,0:T(2,128)(2,1)}), bf16[64,2,1024]{2,1,0:T(2,128)(2,1)S(1)}, u32[]{:S(2)}, u32[]{:S(2)}) async-start(bf16[64,2,1024]{2,1,0:T(2,128)(2,1)} %reshape.879), calls=%async_computation.1 | async-start | bytes 524288 | tf_op jit(solution)/shard_map/all_to_all | solution.py:200
  60.3 51.6 %copy-start.17 = (bf16[1,1024,128]{2,1,0:T(8,128)(2,1)S(1)}, bf16[1,1024,128]{2,1,0:T(8,128)(2,1)}, u32[]{:S(2)}) copy-start(bf16[1,1024,128]{2,1,0:T(8,128)(2,1)} %param.14) | copy-start | bytes 786436
  110.9 1.0 copy-start.8
  116.8 22.9 %all-to-all-start.3 = ((bf16[64,2,1024]{2,1,0:T(2,128)(2,1)}), bf16[64,2,1024]{2,1,0:T(2,128)(2,1)}, u32[]{:S(2)}, u32[]{:S(2)}) async-start(bf16[64,2,1024]{2,1,0:T(2,128)(2,1)} %reshape.883), calls=%async_computation.3 | async-start | bytes 524288 | tf_op jit(solution)/shard_map/all_to_all | solution.py:201
  130.3 1.1 copy-start.11
  130.6 0.9 copy-start.13
  133.2 26.6 %copy-start.1 = (f32[1,16,64,256]{3,2,1,0:T(8,128)}, f32[1,16,64,256]{3,2,1,0:T(8,128)S(1)}, u32[]{:S(2)}) copy-start(f32[1,16,64,256]{3,2,1,0:T(8,128)S(1)} %convolution_bitcast_fusion.2) | copy-start | bytes 3145732
  149.5 6.3 copy-start.3
  162.0 4.0 copy-start.2
  169.9 6.2 copy-start.14
  169.9 7.1 %copy-start.12 = (bf16[1024,1,128]{2,1,0:T(2,128)(2,1)S(1)}, bf16[1024,1,128]{2,1,0:T(2,128)(2,1)}, u32[]{:S(2)}) copy-start(bf16[1024,1,128]{2,1,0:T(2,128)(2,1)} %copy-done.11) | copy-start | bytes 786436
  194.4 60.0 %copy-start.10 = (f32[16,64,256]{2,1,0:T(8,128)S(1)}, f32[16,64,256]{2,1,0:T(8,128)}, u32[]{:S(2)}) copy-start(f32[16,64,256]{2,1,0:T(8,128)} %get-tuple-element.447) | copy-start | bytes 3145732
  245.9 85.7 %all-to-all-start.2 = ((bf16[64,2,1024]{2,1,0:T(2,128)(2,1)}), bf16[64,2,1024]{2,1,0:T(2,128)(2,1)S(1)}, u32[]{:S(2)}, u32[]{:S(2)}) async-start(bf16[64,2,1024]{2,1,0:T(2,128)(2,1)} %reshape.881), calls=%async_computation.2 | async-start | bytes 524288 | tf_op jit(solution)/shard_map/all_to_all | solution.py:214
  261.7 3.6 copy-start.15
  262.6 5.3 copy-start.16
  280.3 64.8 %copy-start = (f32[16,64,256]{2,1,0:T(8,128)S(1)}, f32[16,64,256]{2,1,0:T(8,128)}, u32[]{:S(2)}) copy-start(f32[16,64,256]{2,1,0:T(8,128)} %get-tuple-element.632) | copy-start | bytes 3145732
  280.3 64.8 %copy-start.35 = (f32[16,16]{1,0:T(8,128)S(1)}, f32[16,16]{1,0:T(8,128)}, u32[]{:S(2)}) copy-start(f32[16,16]{1,0:T(8,128)} %custom-call.2) | copy-start | bytes 3076
  280.3 64.8 %copy-start.36 = (f32[16,16]{1,0:T(8,128)S(1)}, f32[16,16]{1,0:T(8,128)}, u32[]{:S(2)}) copy-start(f32[16,16]{1,0:T(8,128)} %custom-call.3) | copy-start | bytes 3076
  331.6 156.5 %all-to-all-start.4 = ((bf16[64,2,1024]{2,1,0:T(2,128)(2,1)}), bf16[64,2,1024]{2,1,0:T(2,128)(2,1)}, u32[]{:S(2)}, u32[]{:S(2)}) async-start(bf16[64,2,1024]{2,1,0:T(2,128)(2,1)} %reshape.885), calls=%async_computation.4 | async-start | bytes 524288 | tf_op jit(solution)/shard_map/all_to_all | solution.py:215
  488.1 32.2 %all-to-all-start.5 = ((bf16[64,2,1024]{2,1,0:T(2,128)(2,1)}), bf16[64,2,1024]{2,1,0:T(2,128)(2,1)S(1)}, u32[]{:S(2)}, u32[]{:S(2)}) async-start(bf16[64,2,1024]{2,1,0:T(2,128)(2,1)} %reshape.887), calls=%async_computation.5 | async-start | bytes 524288 | tf_op jit(solution)/shard_map/all_to_all | solution.py:216
  501.5 18.0 %copy-start.5 = (f32[1,1024,130]{2,1,0:T(8,128)S(1)}, f32[1,1024,130]{2,1,0:T(8,128)}, u32[]{:S(2)}) copy-start(f32[1,1024,130]{2,1,0:T(8,128)} %copy-done.4) | copy-start | bytes 1597444
  520.3 15.9 %copy-start.7 = (f32[1,1024,130]{2,1,0:T(8,128)S(1)}, f32[1,1024,130]{2,1,0:T(8,128)}, u32[]{:S(2)}) copy-start(f32[1,1024,130]{2,1,0:T(8,128)} %copy-done.6) | copy-start | bytes 1597444
  528.0 9.1 %copy-start.9 = (f32[1,1024,130]{2,1,0:T(8,128)S(1)}, f32[1,1024,130]{2,1,0:T(8,128)}, u32[]{:S(2)}) copy-start(f32[1,1024,130]{2,1,0:T(8,128)} %copy-done.8) | copy-start | bytes 1597444
  528.0 9.1 %copy-start.18 = (bf16[1,1024,128]{2,1,0:T(8,128)(2,1)S(1)}, bf16[1,1024,128]{2,1,0:T(8,128)(2,1)}, u32[]{:S(2)}) copy-start(bf16[1,1024,128]{2,1,0:T(8,128)(2,1)} %param.14) | copy-start | bytes 786436
  536.0 96.0 %copy-start.28 = (f32[1,1,1024]{2,1,0:T(1,128)S(1)}, f32[1,1,1024]{2,1,0:T(1,128)}, u32[]{:S(2)}) copy-start(f32[1,1,1024]{2,1,0:T(1,128)} %copy-done.27) | copy-start | bytes 12292
  536.0 96.0 %copy-start.30 = (f32[1,1,1024]{2,1,0:T(1,128)S(1)}, f32[1,1,1024]{2,1,0:T(1,128)}, u32[]{:S(2)}) copy-start(f32[1,1,1024]{2,1,0:T(1,128)} %copy-done.29) | copy-start | bytes 12292
  536.0 96.0 %copy-start.32 = (f32[1,1,1024]{2,1,0:T(1,128)S(1)}, f32[1,1,1024]{2,1,0:T(1,128)}, u32[]{:S(2)}) copy-start(f32[1,1,1024]{2,1,0:T(1,128)} %copy-done.31) | copy-start | bytes 12292
  537.0 99.4 %copy-start.22 = (f32[1,1,1024]{2,1,0:T(1,128)S(1)}, f32[1,1,1024]{2,1,0:T(1,128)}, u32[]{:S(2)}) copy-start(f32[1,1,1024]{2,1,0:T(1,128)} %copy-done.21) | copy-start | bytes 12292
  537.1 99.4 %copy-start.24 = (f32[1,1,1024]{2,1,0:T(1,128)S(1)}, f32[1,1,1024]{2,1,0:T(1,128)}, u32[]{:S(2)}) copy-start(f32[1,1,1024]{2,1,0:T(1,128)} %copy-done.23) | copy-start | bytes 12292
  537.1 99.4 %copy-start.26 = (f32[1,1,1024]{2,1,0:T(1,128)S(1)}, f32[1,1,1024]{2,1,0:T(1,128)}, u32[]{:S(2)}) copy-start(f32[1,1,1024]{2,1,0:T(1,128)} %copy-done.25) | copy-start | bytes 12292
  615.1 16.8 %collective-permute-start.5 = (bf16[1,1024,2]{2,1,0:T(8,128)(2,1)S(1)}, bf16[1,1024,2]{2,1,0:T(8,128)(2,1)S(1)}, u32[]{:S(2)}, u32[]{:S(2)}) collective-permute-start(bf16[1,1024,2]{2,1,0:T(8,128)(2,1)S(1)} %bitcast.321), channel_id=1, source_target_pairs={{1,0},{2,1},{3,2},{4,3},{5,4},{6,5},{7,6},{8,7},{9,8},{10,9},{11,1... | collective-permute-start | bytes 12296 | tf_op jit(solution)/shard_map/ppermute | solution.py:13
  617.6 18.8 %collective-permute-start.4 = (bf16[1,1024,2]{2,1,0:T(8,128)(2,1)S(1)}, bf16[1,1024,2]{2,1,0:T(8,128)(2,1)S(1)}, u32[]{:S(2)}, u32[]{:S(2)}) collective-permute-start(bf16[1,1024,2]{2,1,0:T(8,128)(2,1)S(1)} %bitcast.318), channel_id=1, source_target_pairs={{1,0},{2,1},{3,2},{4,3},{5,4},{6,5},{7,6},{8,7},{9,8},{10,9},{11,1... | collective-permute-start | bytes 12296 | tf_op jit(solution)/shard_map/ppermute | solution.py:13
  621.1 16.9 %collective-permute-start.3 = (bf16[1,1024,2]{1,2,0:T(2,128)(2,1)S(1)}, bf16[1,1024,2]{1,2,0:T(2,128)(2,1)S(1)}, u32[]{:S(2)}, u32[]{:S(2)}) collective-permute-start(bf16[1,1024,2]{1,2,0:T(2,128)(2,1)S(1)} %copy.217), channel_id=1, source_target_pairs={{1,0},{2,1},{3,2},{4,3},{5,4},{6,5},{7,6},{8,7},{9,8},{10,9},{11,1... | collective-permute-start | bytes 12296 | tf_op jit(solution)/shard_map/ppermute | solution.py:13
where the time goes:
time: 652 us; the launch traced here: 640 us
  other arithmetic  289 us (44%)
  local copies, waits for them, and re-layouts  99 us (15%)
  starting transfers between devices  91.3 us (14%)
  blocking collectives  85.8 us (13%)
  matrix products  48.9 us (8%)
  waiting for transfers between devices  22.9 us (4%)
    unnamed x9, other arithmetic  146 us
    psum x1, blocking collectives, per_device(): tap_total = lax.psum(tap_part, ('dp', 'context'))  75.4 us
    unnamed x93, local copies, waits for them, and re-layouts  48.6 us
    dot_general x16, matrix products, along_cols(): jnp.einsum('bckm,mj->bckj', array, table, precision=HIGHEST_PRECISION)  38.5 us
    reduce_sum x16, other arithmetic, one_mode(): jnp.sum(adj_re * tangents[0] + adj_im * tangents[1], axis=(1, 2))  35.3 us
    ppermute x6, waiting for transfers between devices, passed_along(): return lax.ppermute(x, axis, pairs)  18.1 us
    ppermute x6, starting transfers between devices, passed_along(): return lax.ppermute(x, axis, pairs)  18 us
    add x16, other arithmetic, add_mode(): carry[1] + weight_col * resp_im  16.5 us
  transfers between devices with their start and end apart: 12, of which 4 were waited for; matrix products, arithmetic and copies ran while one was open for 47% of the time, Pallas kernels for 0%

commit v1 on v0

--- a/solution.py
+++ b/solution.py
@@ -251,7 +251,7 @@
     token_scale = 1.0 / math.sqrt(
         queries.shape[0] * lax.axis_size("dp") * length_here * lax.axis_size("context")
     )
-    tap_total = lax.psum(tap_part, ("dp", "context"))
+    tap_total = lax.psum(lax.psum(tap_part, "context"), "dp")
     residue_own, decay_own = lax.psum((residue_adj, decay_adj), "dp")
     return (
         output,

time: 652 us -> 948 us (1.45)
  blocking collectives: 85.8 us -> 362 us
  local copies, waits for them, and re-layouts: 99 us -> 115 us
    psum x2, blocking collectives: 85.8 us -> 362 us  [per_device(): tap_total = lax.psum(lax.psum(tap_part, 'context'), 'dp')]
    dynamic_update_slice x32, local copies, waits for them, and re-layouts: 0.86 us -> 20.8 us  [mode_adjoints(): lax.scan(one_mode, jnp.zeros((), jnp.float32), (residues.T, decay_rates.T))]
    unnamed x93 -> x95, local copies, waits for them, and re-layouts: 48.6 us -> 45.1 us
  transfers between devices with their start and end apart: 12 -> 12, of which waited for: 4 -> 5; matrix products, arithmetic and copies ran while one was open for 47% -> 20% of each run, Pallas kernels for 0% -> 0%
where the time goes in v1:
time: 948 us; the launch traced here: 931 us
  blocking collectives  362 us (38%)
  other arithmetic  285 us (30%)
  local copies, waits for them, and re-layouts  115 us (12%)
  starting transfers between devices  86.9 us (9%)
  matrix products  51.7 us (5%)
  waiting for transfers between devices  26.4 us (3%)
    psum x2, blocking collectives, per_device(): tap_total = lax.psum(lax.psum(tap_part, 'context'), 'dp')  362 us
    unnamed x9, other arithmetic  144 us
    unnamed x95, local copies, waits for them, and re-layouts  45.1 us
    dot_general x16, matrix products, along_cols(): jnp.einsum('bckm,mj->bckj', array, table, precision=HIGHEST_PRECISION)  41.5 us
    reduce_sum x16, other arithmetic, one_mode(): jnp.sum(adj_re * tangents[0] + adj_im * tangents[1], axis=(1, 2))  35.3 us
    dynamic_update_slice x32, local copies, waits for them, and re-layouts, mode_adjoints(): lax.scan(one_mode, jnp.zeros((), jnp.float32), (residues.T, decay_rates.T))  20.8 us
  transfers between devices with their start and end apart: 12, of which 5 were waited for; matrix products, arithmetic and copies ran while one was open for 20% of the time, Pallas kernels for 0%

profile of v1, /device:TPU:230, one launch (start us, length us, event | category | flops | bytes accessed | tf_op | source)
XLA Modules:
  0.0 930.6 jit_solution(18262843994272065466)
XLA Ops:
  4.7 7.0 collective-permute-done.1
  18.6 12.4 %all-to-all-start = ((bf16[64,2,1024]{2,1,0:T(2,128)(2,1)}), bf16[64,2,1024]{2,1,0:T(2,128)(2,1)S(1)}, u32[]{:S(2)}, u32[]{:S(2)}) async-start(bf16[64,2,1024]{2,1,0:T(2,128)(2,1)} %reshape.877), calls=%async_computation | async-start | bytes 524288 | tf_op jit(solution)/shard_map/all_to_all | solution.py:199
  31.9 4.9 collective-permute-start
  36.9 3.4 collective-permute-start.2
  41.7 3.5 collective-permute-done.2
  47.6 2.2 reduce.1
  50.5 12.6 %all-to-all-start.1 = ((bf16[64,2,1024]{2,1,0:T(2,128)(2,1)}), bf16[64,2,1024]{2,1,0:T(2,128)(2,1)S(1)}, u32[]{:S(2)}, u32[]{:S(2)}) async-start(bf16[64,2,1024]{2,1,0:T(2,128)(2,1)} %reshape.879), calls=%async_computation.1 | async-start | bytes 524288 | tf_op jit(solution)/shard_map/all_to_all | solution.py:200
  63.1 48.0 %while.33 = (s32[]{:T(128)}, f32[16,64,256]{2,1,0:T(8,128)S(1)}, f32[16,64,256]{2,1,0:T(8,128)S(1)}, f32[16,16]{1,0:T(8,128)}, f32[16,16]{1,0:T(8,128)}, /*index=5*/s32[256]{0:T(256)S(1)}, s32[]{:T(128)}, s32[]{:T(128)}) while((s32[]{:T(128)}, f32[16,64,256]{2,1,0:T(8,128)S(1)}, ...), condition=%wide.region_1.2_spmd.clone.clone.clone, body=%wide.region_0.1_spmd.clone.clone.clone.sunk | while | flops 5062803 | bytes 4492591 | solution.py:113
  115.4 2.2 reduce.2
  118.6 13.0 %all-to-all-start.3 = ((bf16[64,2,1024]{2,1,0:T(2,128)(2,1)}), bf16[64,2,1024]{2,1,0:T(2,128)(2,1)}, u32[]{:S(2)}, u32[]{:S(2)}) async-start(bf16[64,2,1024]{2,1,0:T(2,128)(2,1)} %reshape.883), calls=%async_computation.3 | async-start | bytes 524288 | tf_op jit(solution)/shard_map/all_to_all | solution.py:201
  133.7 7.8 all-to-all-done.3
  141.5 2.7 reshape.884
  148.0 3.1 convolution_bitcast_fusion.1
  160.4 2.2 fusion.62
  168.6 4.7 multiply_add_fusion.3
  173.3 2.9 fusion.77
  176.3 3.0 fusion.132
  179.3 88.0 %while.32 = (s32[]{:T(128)}, f32[16,16]{1,0:T(8,128)S(1)}, f32[16,16]{1,0:T(8,128)}, f32[16,16]{1,0:T(8,128)}, f32[16,64,256]{2,1,0:T(8,128)S(1)}, /*index=5*/f3...) while((s32[]{:T(128)}, f32[16,16]{1,0:T(8,128)S(1)}, ...), condition=%wide.region_16.17_spmd.clone.clone.clone, body=%wide.region_13.16_spmd.clone.clone.clone.sunk | while | flops 12403026 | bytes 2396669 | solution.py:136
  180.6 2.2 fusion.310
  186.1 2.2 fusion.310
  191.5 2.2 fusion.310
  197.0 2.2 fusion.310
  202.4 2.2 fusion.310
  207.9 2.2 fusion.310
  213.4 2.2 fusion.310
  218.8 2.2 fusion.310
  224.3 2.2 fusion.310
  229.8 2.2 fusion.310
  235.2 2.2 fusion.310
  240.7 2.2 fusion.310
  246.2 2.2 fusion.310
  251.7 2.2 fusion.310
  257.1 2.2 fusion.310
  262.6 2.2 fusion.310
  267.2 3.2 convolution_add_fusion
  270.4 3.3 convolution_add_fusion.1
  275.6 3.0 fusion.136
  278.7 2.6 copy.231
  281.3 2.6 copy.221
  283.9 2.6 copy.225
  286.5 9.7 %multiply_convert_fusion = (bf16[1,16,8192]{1,0,2:T(2,128)(2,1)}, bf16[1,16,8192]{1,0,2:T(2,128)(2,1)}) fusion(f32[1,16,8192]{1,0,2:T(1,128)} %bitcast.306, f32[1,16,8192]{1,0,2:T(1,128)} %bitcast.308, f32[1,16,8192]{1,0,2:T(1,128)} %bitcast.307), kind=kLoop, calls=%fused_computation.90 | loop fusion | flops 524288 | bytes 2097152 | tf_op jit(solution)/shard_map/convert_element_type | solution.py:210
  296.2 45.4 %reduce.5 = bf16[8192,16]{1,0:T(8,128)(2,1)S(1)} reduce(bf16[8192,1,16]{2,1,0:T(2,128)(2,1)} %bitcast.309, bf16[]{:T(256)} %broadcast.596), dimensions={1}, to_apply=%bitcast.259.reduce_sub_computation | reduce | bytes 524290
  341.6 2.9 reshape.887
  344.5 46.8 %reduce.4 = bf16[8192,16]{1,0:T(8,128)(2,1)} reduce(bf16[8192,1,16]{2,1,0:T(2,128)(2,1)} %bitcast.305, bf16[]{:T(256)} %broadcast.596), dimensions={1}, to_apply=%bitcast.257.reduce_sub_computation | reduce | bytes 524290
  391.4 4.4 reshape.885
  395.7 8.2 all-to-all-start.5
  403.9 3.2 convolution_add_fusion.4
  411.1 2.8 all-to-all-done.5
  414.6 10.5 %all-to-all-start.4 = ((bf16[64,2,1024]{2,1,0:T(2,128)(2,1)}), bf16[64,2,1024]{2,1,0:T(2,128)(2,1)S(1)}, u32[]{:S(2)}, u32[]{:S(2)}) async-start(bf16[64,2,1024]{2,1,0:T(2,128)(2,1)} %reshape.885), calls=%async_computation.4 | async-start | bytes 524288 | tf_op jit(solution)/shard_map/all_to_all | solution.py:215
  429.8 6.7 copy.214
  436.5 45.2 %reduce.3 = bf16[8192,16]{1,0:T(8,128)(2,1)S(1)} reduce(bf16[8192,1,16]{2,1,0:T(2,128)(2,1)} %bitcast.310, bf16[]{:T(256)} %broadcast.596), dimensions={1}, to_apply=%bitcast.253.reduce_sub_computation | reduce | bytes 524290
  481.7 2.9 reshape.881
  484.6 7.6 reshape.888
  492.2 7.9 copy.227
  500.4 2.8 collective-permute-start.5
  503.1 12.5 %all-to-all-start.2 = ((bf16[64,2,1024]{2,1,0:T(2,128)(2,1)}), bf16[64,2,1024]{2,1,0:T(2,128)(2,1)S(1)}, u32[]{:S(2)}, u32[]{:S(2)}) async-start(bf16[64,2,1024]{2,1,0:T(2,128)(2,1)} %reshape.881), calls=%async_computation.2 | async-start | bytes 524288 | tf_op jit(solution)/shard_map/all_to_all | solution.py:214
  515.7 7.6 reshape.886
  523.3 8.0 copy.223
  531.5 2.9 collective-permute-start.4
  536.0 7.6 reshape.882
  543.6 8.0 copy.215
  553.7 350.7 %psum.28 = f32[3,3,1024]{2,1,0:T(4,128)S(1)} all-reduce(f32[3,3,1024]{2,1,0:T(4,128)S(1)} %pad_maximum_fusion), channel_id=1, replica_groups=mesh['dp'=4,'context'=64] {'context'}, use_global_device_ids=true, to_apply=%region_11.12 | all-reduce | flops 9216 | bytes 73728 | tf_op jit(solution)/shard_map/psum | solution.py:254
  904.4 11.1 %all-reduce = (f32[3,3,1024]{2,1,0:T(4,128)S(1)}, f32[16,16]{1,0:T(8,128)S(1)}, f32[16,16]{1,0:T(8,128)S(1)}) all-reduce(f32[3,3,1024]{2,1,0:T(4,128)S(1)} %psum.28, f32[16,16]{1,0:T(8,128)S(1)} %bitcast.356, f32[16,16]{1,0:T(8,128)S(1)} %bitcast.355), channel_id=1, replica_groups=mesh['dp'=4,'context'=64] {'dp'}, use_global_device_ids=true, to_apply=%region_12.13 | all-reduce | flops 9728 | bytes 77824 | tf_op jit(solution)/shard_map/psum | solution.py:254
  923.5 5.2 collective-permute-done.3
  (392 shorter events, 166.3 us)
Async XLA Ops:
  0.6 30.4 %copy-start.19 = (bf16[1,1024,128]{2,1,0:T(8,128)(2,1)S(1)}, bf16[1,1024,128]{2,1,0:T(8,128)(2,1)}, u32[]{:S(2)}) copy-start(bf16[1,1024,128]{2,1,0:T(8,128)(2,1)} %param.11) | copy-start | bytes 786436
  0.6 36.1 %copy-start.18 = (bf16[1,1024,128]{2,1,0:T(8,128)(2,1)S(1)}, bf16[1,1024,128]{2,1,0:T(8,128)(2,1)}, u32[]{:S(2)}) copy-start(bf16[1,1024,128]{2,1,0:T(8,128)(2,1)} %param.13) | copy-start | bytes 786436
  0.7 39.7 %copy-start.34 = (f32[16,16]{1,0:T(8,128)S(1)}, f32[16,16]{1,0:T(8,128)}, u32[]{:S(2)}) copy-start(f32[16,16]{1,0:T(8,128)} %param.16) | copy-start | bytes 3076
  0.7 40.3 %copy-start.35 = (f32[16,16]{1,0:T(8,128)S(1)}, f32[16,16]{1,0:T(8,128)}, u32[]{:S(2)}) copy-start(f32[16,16]{1,0:T(8,128)} %param.17) | copy-start | bytes 3076
  1.8 9.9 %collective-permute-start.1 = (bf16[1,1024,2]{2,1,0:T(8,128)(2,1)S(1)}, bf16[1,1024,2]{2,1,0:T(8,128)(2,1)S(1)}, u32[]{:S(2)}, u32[]{:S(2)}) collective-permute-start(bf16[1,1024,2]{2,1,0:T(8,128)(2,1)S(1)} %slice.146), channel_id=1, source_target_pairs={{0,1},{1,2},{2,3},{3,4},{4,5},{5,6},{6,7},{7,8},{8,9},{9,10},{10,1... | collective-permute-start | bytes 12296 | tf_op jit(solution)/shard_map/ppermute | solution.py:13
  4.7 13.9 %copy-start.20 = (f32[1,1,1024]{2,1,0:T(1,128)}, f32[1,1,1024]{2,1,0:T(1,128)S(1)}, u32[]{:S(2)}) copy-start(f32[1,1,1024]{2,1,0:T(1,128)S(1)} %get-tuple-element.453) | copy-start | bytes 12292
  4.7 13.9 %copy-start.22 = (f32[1,1,1024]{2,1,0:T(1,128)}, f32[1,1,1024]{2,1,0:T(1,128)S(1)}, u32[]{:S(2)}) copy-start(f32[1,1,1024]{2,1,0:T(1,128)S(1)} %get-tuple-element.454) | copy-start | bytes 12292
  4.7 13.9 %copy-start.24 = (f32[1,1,1024]{2,1,0:T(1,128)}, f32[1,1,1024]{2,1,0:T(1,128)S(1)}, u32[]{:S(2)}) copy-start(f32[1,1,1024]{2,1,0:T(1,128)S(1)} %get-tuple-element.455) | copy-start | bytes 12292
  4.7 40.7 %copy-start.26 = (f32[1,1,1024]{2,1,0:T(1,128)}, f32[1,1,1024]{2,1,0:T(1,128)S(1)}, u32[]{:S(2)}) copy-start(f32[1,1,1024]{2,1,0:T(1,128)S(1)} %get-tuple-element.452) | copy-start | bytes 12292
  4.7 40.7 %copy-start.28 = (f32[1,1,1024]{2,1,0:T(1,128)}, f32[1,1,1024]{2,1,0:T(1,128)S(1)}, u32[]{:S(2)}) copy-start(f32[1,1,1024]{2,1,0:T(1,128)S(1)} %get-tuple-element.459) | copy-start | bytes 12292
  4.7 40.7 %copy-start.30 = (f32[1,1,1024]{2,1,0:T(1,128)}, f32[1,1,1024]{2,1,0:T(1,128)S(1)}, u32[]{:S(2)}) copy-start(f32[1,1,1024]{2,1,0:T(1,128)S(1)} %get-tuple-element.460) | copy-start | bytes 12292
  12.9 1.0 copy-start.2
  18.6 31.9 %all-to-all-start = ((bf16[64,2,1024]{2,1,0:T(2,128)(2,1)}), bf16[64,2,1024]{2,1,0:T(2,128)(2,1)S(1)}, u32[]{:S(2)}, u32[]{:S(2)}) async-start(bf16[64,2,1024]{2,1,0:T(2,128)(2,1)} %reshape.877), calls=%async_computation | async-start | bytes 524288 | tf_op jit(solution)/shard_map/all_to_all | solution.py:199
  31.9 79.5 %collective-permute-start = (bf16[1,1024,2]{1,2,0:T(2,128)(2,1)}, bf16[1,1024,2]{1,2,0:T(2,128)(2,1)}, u32[]{:S(2)}, u32[]{:S(2)}) collective-permute-start(bf16[1,1024,2]{1,2,0:T(2,128)(2,1)} %copy.232), channel_id=1, source_target_pairs={{0,1},{1,2},{2,3},{3,4},{4,5},{5,6},{6,7},{7,8},{8,9},{9,10},{10,1... | collective-permute-start | bytes 12296 | tf_op jit(solution)/shard_map/ppermute | solution.py:13
  36.9 8.3 collective-permute-start.2
  45.4 1.0 copy-start.4
  50.5 68.1 %all-to-all-start.1 = ((bf16[64,2,1024]{2,1,0:T(2,128)(2,1)}), bf16[64,2,1024]{2,1,0:T(2,128)(2,1)S(1)}, u32[]{:S(2)}, u32[]{:S(2)}) async-start(bf16[64,2,1024]{2,1,0:T(2,128)(2,1)} %reshape.879), calls=%async_computation.1 | async-start | bytes 524288 | tf_op jit(solution)/shard_map/all_to_all | solution.py:200
  63.1 50.4 %copy-start.13 = (bf16[1,1024,128]{2,1,0:T(8,128)(2,1)S(1)}, bf16[1,1024,128]{2,1,0:T(8,128)(2,1)}, u32[]{:S(2)}) copy-start(bf16[1,1024,128]{2,1,0:T(8,128)(2,1)} %param.14) | copy-start | bytes 786436
  112.5 1.0 copy-start.6
  118.6 22.9 %all-to-all-start.3 = ((bf16[64,2,1024]{2,1,0:T(2,128)(2,1)}), bf16[64,2,1024]{2,1,0:T(2,128)(2,1)}, u32[]{:S(2)}, u32[]{:S(2)}) async-start(bf16[64,2,1024]{2,1,0:T(2,128)(2,1)} %reshape.883), calls=%async_computation.3 | async-start | bytes 524288 | tf_op jit(solution)/shard_map/all_to_all | solution.py:201
  153.6 4.7 copy-start.1
  173.3 5.9 copy-start
  173.3 5.9 copy-start.36
  179.3 88.0 %copy-start.8 = (f32[16,64,256]{2,1,0:T(8,128)S(1)}, f32[16,64,256]{2,1,0:T(8,128)}, u32[]{:S(2)}) copy-start(f32[16,64,256]{2,1,0:T(8,128)} %get-tuple-element.448) | copy-start | bytes 3145732
  267.2 7.4 copy-start.37
  270.4 5.2 copy-start.9
  275.6 5.7 copy-start.12
  278.6 5.3 copy-start.11
  344.5 59.4 %copy-start.10 = (f32[16,64,256]{2,1,0:T(8,128)S(1)}, f32[16,64,256]{2,1,0:T(8,128)}, u32[]{:S(2)}) copy-start(f32[16,64,256]{2,1,0:T(8,128)} %get-tuple-element.450) | copy-start | bytes 3145732
  395.7 18.1 %all-to-all-start.5 = ((bf16[64,2,1024]{2,1,0:T(2,128)(2,1)}), bf16[64,2,1024]{2,1,0:T(2,128)(2,1)S(1)}, u32[]{:S(2)}, u32[]{:S(2)}) async-start(bf16[64,2,1024]{2,1,0:T(2,128)(2,1)} %reshape.887), calls=%async_computation.5 | async-start | bytes 524288 | tf_op jit(solution)/shard_map/all_to_all | solution.py:216
  413.9 0.7 copy-start.16
  414.6 88.5 %all-to-all-start.4 = ((bf16[64,2,1024]{2,1,0:T(2,128)(2,1)}), bf16[64,2,1024]{2,1,0:T(2,128)(2,1)S(1)}, u32[]{:S(2)}, u32[]{:S(2)}) async-start(bf16[64,2,1024]{2,1,0:T(2,128)(2,1)} %reshape.885), calls=%async_computation.4 | async-start | bytes 524288 | tf_op jit(solution)/shard_map/all_to_all | solution.py:215
  436.4 48.2 %copy-start.17 = (bf16[64,2,1024]{2,1,0:T(2,128)(2,1)S(1)}, bf16[64,2,1024]{2,1,0:T(2,128)(2,1)}, u32[]{:S(2)}) copy-start(bf16[64,2,1024]{2,1,0:T(2,128)(2,1)} %copy-done.16) | copy-start | bytes 786436
  500.4 419.0 %collective-permute-start.5 = (bf16[1,1024,2]{2,1,0:T(8,128)(2,1)S(1)}, bf16[1,1024,2]{2,1,0:T(8,128)(2,1)}, u32[]{:S(2)}, u32[]{:S(2)}) collective-permute-start(bf16[1,1024,2]{2,1,0:T(8,128)(2,1)S(1)} %bitcast.318), channel_id=1, source_target_pairs={{1,0},{2,1},{3,2},{4,3},{5,4},{6,5},{7,6},{8,7},{9,8},{10,9},{11,1... | collective-permute-start | bytes 12296 | tf_op jit(solution)/shard_map/ppermute | solution.py:13
  503.1 32.9 %all-to-all-start.2 = ((bf16[64,2,1024]{2,1,0:T(2,128)(2,1)}), bf16[64,2,1024]{2,1,0:T(2,128)(2,1)S(1)}, u32[]{:S(2)}, u32[]{:S(2)}) async-start(bf16[64,2,1024]{2,1,0:T(2,128)(2,1)} %reshape.881), calls=%async_computation.2 | async-start | bytes 524288 | tf_op jit(solution)/shard_map/all_to_all | solution.py:214
  515.7 18.8 %copy-start.5 = (f32[1,1024,130]{2,1,0:T(8,128)S(1)}, f32[1,1024,130]{2,1,0:T(8,128)}, u32[]{:S(2)}) copy-start(f32[1,1024,130]{2,1,0:T(8,128)} %copy-done.4) | copy-start | bytes 1597444
  523.3 11.9 %copy-start.3 = (f32[1,1024,130]{2,1,0:T(8,128)S(1)}, f32[1,1024,130]{2,1,0:T(8,128)}, u32[]{:S(2)}) copy-start(f32[1,1024,130]{2,1,0:T(8,128)} %copy-done.2) | copy-start | bytes 1597444
  531.5 390.4 %collective-permute-start.4 = (bf16[1,1024,2]{2,1,0:T(8,128)(2,1)S(1)}, bf16[1,1024,2]{2,1,0:T(8,128)(2,1)S(1)}, u32[]{:S(2)}, u32[]{:S(2)}) collective-permute-start(bf16[1,1024,2]{2,1,0:T(8,128)(2,1)S(1)} %bitcast.320), channel_id=1, source_target_pairs={{1,0},{2,1},{3,2},{4,3},{5,4},{6,5},{7,6},{8,7},{9,8},{10,9},{11,1... | collective-permute-start | bytes 12296 | tf_op jit(solution)/shard_map/ppermute | solution.py:13
  543.6 8.5 copy-start.7
  543.6 8.5 copy-start.14
  543.6 8.5 copy-start.15
  551.6 352.7 %copy-start.32 = (f32[16,16]{0,1:T(8,128)S(1)}, f32[16,16]{0,1:T(8,128)}, u32[]{:S(2)}) copy-start(f32[16,16]{0,1:T(8,128)} %copy.230) | copy-start | bytes 3076
  551.6 352.7 %copy-start.33 = (f32[16,16]{0,1:T(8,128)S(1)}, f32[16,16]{0,1:T(8,128)}, u32[]{:S(2)}) copy-start(f32[16,16]{0,1:T(8,128)} %copy.229) | copy-start | bytes 3076
  551.7 368.8 %copy-start.27 = (f32[1,1,1024]{2,1,0:T(1,128)S(1)}, f32[1,1,1024]{2,1,0:T(1,128)}, u32[]{:S(2)}) copy-start(f32[1,1,1024]{2,1,0:T(1,128)} %copy-done.26) | copy-start | bytes 12292
  551.7 368.8 %copy-start.29 = (f32[1,1,1024]{2,1,0:T(1,128)S(1)}, f32[1,1,1024]{2,1,0:T(1,128)}, u32[]{:S(2)}) copy-start(f32[1,1,1024]{2,1,0:T(1,128)} %copy-done.28) | copy-start | bytes 12292
  551.7 368.8 %copy-start.31 = (f32[1,1,1024]{2,1,0:T(1,128)S(1)}, f32[1,1,1024]{2,1,0:T(1,128)}, u32[]{:S(2)}) copy-start(f32[1,1,1024]{2,1,0:T(1,128)} %copy-done.30) | copy-start | bytes 12292
  552.2 369.8 %copy-start.21 = (f32[1,1,1024]{2,1,0:T(1,128)S(1)}, f32[1,1,1024]{2,1,0:T(1,128)}, u32[]{:S(2)}) copy-start(f32[1,1,1024]{2,1,0:T(1,128)} %copy-done.20) | copy-start | bytes 12292
  552.2 369.8 %copy-start.23 = (f32[1,1,1024]{2,1,0:T(1,128)S(1)}, f32[1,1,1024]{2,1,0:T(1,128)}, u32[]{:S(2)}) copy-start(f32[1,1,1024]{2,1,0:T(1,128)} %copy-done.22) | copy-start | bytes 12292
  552.2 369.8 %copy-start.25 = (f32[1,1,1024]{2,1,0:T(1,128)S(1)}, f32[1,1,1024]{2,1,0:T(1,128)}, u32[]{:S(2)}) copy-start(f32[1,1,1024]{2,1,0:T(1,128)} %copy-done.24) | copy-start | bytes 12292
  917.5 11.2 %collective-permute-start.3 = (bf16[1,1024,2]{1,2,0:T(2,128)(2,1)S(1)}, bf16[1,1024,2]{1,2,0:T(2,128)(2,1)S(1)}, u32[]{:S(2)}, u32[]{:S(2)}) collective-permute-start(bf16[1,1024,2]{1,2,0:T(2,128)(2,1)S(1)} %copy.217), channel_id=1, source_target_pairs={{1,0},{2,1},{3,2},{4,3},{5,4},{6,5},{7,6},{8,7},{9,8},{10,9},{11,1... | collective-permute-start | bytes 12296 | tf_op jit(solution)/shard_map/ppermute | solution.py:13
